TPU v7x, 512 devices: a whole 4x8x8 slice. The times are simulated.
512 devices in a mesh: row: 32 (over x_lo, y, core), col: 16 (over z, x_hi).
Axes of the slice: x: 4 (x_hi: 2, x_lo: 2; x = x_hi * 2 + x_lo), y: 8, z: 8, core: 2. Of those that a mesh axis runs over, the one named last changes fastest.
Arguments:
- support: bfloat16 [131072, 4096], P(('row', 'col')), may hold values from -6 to 6
- targets: bfloat16 [1024, 4096], P('col'), may hold values from -6 to 6
- panels: float32 [2, 128, 131072], P(None, None, ('row', 'col')), may hold values from -0.21875 to 0.21875
- diag_inverses: float32 [2, 128, 128], replicated, may hold values from -1 to 1.5, as said below
Outputs:
- solved: float32 [1024, 131072], P('col', 'row')
Inputs may be any that keep to these rules, and one draw needn't show every extreme that they name: Each diag_inverses[k] is lower triangular.
All inputs are finite; a program needn't handle non-finite values.
Results may differ from a plain program's by a relative error of at most 0.0003.
Values may be sent and summed in bfloat16 or wider, within the bound.
A program may use at most 64 MiB of HBM per device.

v0:
```python
import math

import jax
import jax.numpy as jnp
from jax import lax
from jax.sharding import PartitionSpec as P


def spread(value, axis, root):
    mine = lax.axis_index(axis) == root
    return lax.psum(jnp.where(mine, value, jnp.zeros_like(value)), axis)


def solve_head(pivot_cols, inverse):
    return jnp.dot(
        pivot_cols, inverse.T, precision=lax.Precision.HIGHEST, preferred_element_type=jnp.float32
    )


def apply_panel(current, solved_head, panel_cols):
    return current - jnp.dot(
        solved_head, panel_cols, precision=lax.Precision.HIGHEST, preferred_element_type=jnp.float32
    )


def shards(support, targets, panels, diag_inverses):
    feature_width = support.shape[1]
    kernel_scale = 0.5 / math.sqrt(feature_width)
    pivot_width = diag_inverses.shape[1]
    row_pos = lax.axis_index("row")
    products = jnp.einsum(
        "tf,sf->ts",
        lax.all_gather(targets, "col", axis=0, tiled=True),
        support,
        preferred_element_type=jnp.float32,
    )
    strip_tile = jnp.exp(kernel_scale * products)
    grid_tile = lax.all_to_all(strip_tile, "col", split_axis=0, concat_axis=1, tiled=True)
    panel_grid = lax.all_gather(panels, "col", axis=2, tiled=True)
    for panel_num in range(2):
        pivot_cols = grid_tile[:, :pivot_width]
        solved_head = spread(solve_head(pivot_cols, diag_inverses[panel_num]), "row", panel_num)
        updated = apply_panel(grid_tile, solved_head, panel_grid[panel_num])
        new_head = jnp.where(
            row_pos == panel_num,
            solved_head,
            jnp.where(row_pos < panel_num, pivot_cols, updated[:, :pivot_width]),
        )
        grid_tile = updated.at[:, :pivot_width].set(new_head)
    return grid_tile


def solution(mesh):
    in_specs = (P(("row", "col"), None), P("col", None), P(None, None, ("row", "col")), P())
    out_specs = P("col", "row")
    return jax.shard_map(shards, mesh=mesh, in_specs=in_specs, out_specs=out_specs, check_vma=False)
```

profile of v0, /device:TPU:1, one launch (start us, length us, event | category | flops | bytes accessed | tf_op | source)
XLA Modules:
  0.0 428.7 jit_solution(4030041354875455081)
XLA Ops:
  6.5 0.0 copy-start
  6.5 0.0 all-gather.3.cloned.1.call-start
  6.5 0.7 all-gather.3.cloned.1.call-update
  7.3 0.0 all-gather.5.cloned.1.call-start
  7.3 0.7 all-gather.5.cloned.1.call-update
  8.0 149.5 %all-gather.3.cloned.1.call-done = bf16[1024,4096]{1,0:T(8,128)(2,1)} async-done(((bf16[64,4096]{1,0:T(8,128)(2,1)}), bf16[1024,4096]{1,0:T(8,128)(2,1)}) %all-gather.3.cloned.1.call-update) | async-done | bytes 8388624 | tf_op jit(solution)/shard_map/all_gather | solution.py:33
  157.5 0.0 copy-done
  157.5 6.7 %fusion = f32[1024,256]{1,0:T(8,128)} fusion(bf16[1024,4096]{1,0:T(8,128)(2,1)} %all-gather.3.cloned.1.call-done, bf16[256,4096]{1,0:T(8,128)(2,1)S(1)} %copy-done), kind=kOutput, calls=%fused_computation.5 | convolution fusion | flops 2147745792 | bytes 11534336 | tf_op jit(solution)/shard_map/tf,sf->ts/dot_general | solution.py:31
  164.2 4.1 all-to-all-start
  168.4 0.6 compare_reduce_fusion
  169.0 29.8 %all-to-all-done = f32[16,64,256]{2,1,0:T(8,128)S(1)} async-done(((f32[16,64,256]{2,1,0:T(8,128)}), f32[16,64,256]{2,1,0:T(8,128)S(1)}, u32[]{:S(2)}, u32[]{:S(2)}) %all-to-all-start) | async-done | bytes 1048608 | tf_op jit(solution)/shard_map/all_to_all | solution.py:38
  198.8 1.0 copy-done.2
  199.8 1.3 copy.6
  201.1 0.0 copy-done.3
  201.1 0.2 convolution_select_fusion.1
  201.4 105.4 %psum.14 = f32[64,128]{1,0:T(8,128)S(1)} all-reduce(f32[64,128]{1,0:T(8,128)S(1)} %convolution_select_fusion.1), channel_id=1, replica_groups=mesh['row'=32,'col'=16] {'row'}, use_global_device_ids=true, to_apply=%region_0.1 | all-reduce | flops 8192 | bytes 65536 | tf_op jit(solution)/shard_map/psum | solution.py:11
  306.8 2.8 convolution_subtract_fusion.1
  309.6 0.6 constant_dynamic-update-slice_fusion
  310.2 0.0 copy-start.1
  310.2 1.0 copy-done.1
  311.2 0.2 convolution_select_fusion
  311.5 104.4 %psum.15 = f32[64,128]{1,0:T(8,128)S(1)} all-reduce(f32[64,128]{1,0:T(8,128)S(1)} %convolution_select_fusion), channel_id=1, replica_groups=mesh['row'=32,'col'=16] {'row'}, use_global_device_ids=true, to_apply=%region_2.3 | all-reduce | flops 8192 | bytes 65536 | tf_op jit(solution)/shard_map/psum | solution.py:11
  415.9 4.0 convolution_subtract_fusion
  419.9 2.0 select_dynamic-update-slice_fusion
  (3 shorter events, 0.0 us)
Async XLA Ops:
  6.5 151.0 %copy-start = (bf16[256,4096]{1,0:T(8,128)(2,1)S(1)}, bf16[256,4096]{1,0:T(8,128)(2,1)}, u32[]{:S(2)}) copy-start(bf16[256,4096]{1,0:T(8,128)(2,1)} %param.8) | copy-start | bytes 6291460
  6.5 151.0 %all-gather.3.cloned.1.call-start = ((), (), s32[]{:S(2)}) async-start(), calls=%async_computation.1 | async-start | bytes 8912896 | tf_op jit(solution)/shard_map/all_gather | solution.py:33
  7.3 299.5 %all-gather.5.cloned.1.call-start = ((), (), s32[]{:S(2)}) async-start(), calls=%async_computation.2 | async-start | bytes 4456448 | tf_op jit(solution)/shard_map/all_gather | solution.py:39
  164.2 36.9 %copy-start.3 = (f32[2,128,128]{2,1,0:T(8,128)S(1)}, f32[2,128,128]{2,1,0:T(8,128)}, u32[]{:S(2)}) copy-start(f32[2,128,128]{2,1,0:T(8,128)} %param.11) | copy-start | bytes 393220
  164.2 34.6 %all-to-all-start = ((f32[16,64,256]{2,1,0:T(8,128)}), f32[16,64,256]{2,1,0:T(8,128)S(1)}, u32[]{:S(2)}, u32[]{:S(2)}) async-start(f32[16,64,256]{2,1,0:T(8,128)} %bitcast.25), calls=%async_computation | async-start | bytes 2097152 | tf_op jit(solution)/shard_map/all_to_all | solution.py:38
  198.8 1.0 copy-start.2
  310.2 1.0 copy-start.1
Sparse Core Ops, SparseCore 0:
  10.5 146.9 all-gather.2
  160.6 113.9 all-gather.4
where the time goes:
time: 433 us; the launch traced here: 429 us
  blocking collectives  210 us (48%)
  waiting for transfers between devices  181 us (42%)
  matrix products  14.1 us (3%)
  between operations  13.5 us (3%)
    psum x2, blocking collectives, spread(): return lax.psum(jnp.where(mine, value, jnp.zeros_like(value)), axis)  210 us
    all_gather x1, waiting for transfers between devices, shards(): lax.all_gather(targets, 'col', axis=0, tiled=True)  149 us
    all_to_all x1, waiting for transfers between devices, shards(): lax.all_to_all(strip_tile, 'col', split_axis=0, concat_axis=1, tiled=True)  29.8 us
  transfers between devices with their start and end apart: 3, of which 2 were waited for; matrix products, arithmetic and copies ran while one was open for 2% of the time, Pallas kernels for 0%

commit v1 on v0

v1 whole, which is shorter than its diff:
```python
import math

import jax
import jax.numpy as jnp
from jax import lax
from jax.experimental import pallas as pl
from jax.experimental.pallas import tpu as pltpu
from jax.sharding import PartitionSpec as P

MESH = pl.DeviceIdType.MESH
NZ, NY, NX = 8, 8, 4
BAND = 16
HIGH = lax.Precision.HIGHEST


def dot_t(a, b, precision=None):
    return lax.dot_general(
        a, b, (((1,), (1,)), ((), ())), precision=precision, preferred_element_type=jnp.float32
    )


def body(
    scale, sup, tgt, pan, inv, out,
    full, piv, cross_pan, kern, sol,
    full_recv, z_send, cross_send, part_send, sib_send,
    piv_own, piv_z, piv_x, piv_b, root_send, y_send, pz_send, px_send, pb_send,
    pan_own, pan_z, pan_b, rootp_send, yp_send, pzp_send, pbp_send,
    out_recv, out_send,
):
    row = lax.axis_index("row")
    col = lax.axis_index("col")
    core = row % 2
    y = (row // 2) % NY
    x_lo = row // (2 * NY)
    z = col // 2
    x_hi = col % 2
    x = x_hi * 2 + x_lo
    quarter = sup.shape[1] // NX

    def dev(xx, yy, zz, kk):
        return ((xx % 2) * (2 * NY) + yy * 2 + kk, zz * 2 + xx // 2)

    sibling = dev(x, y, z, 1 - core)
    crossing = dev(NX - 1 - x, y, z, core)
    partner = dev(x_hi * 2 + 1 - x_lo, y, z, core)

    def copy(src, dst, send, recv, to):
        return pltpu.make_async_remote_copy(
            src_ref=src, dst_ref=dst, send_sem=send, recv_sem=recv, device_id=to, device_id_type=MESH
        )

    barrier = pltpu.get_barrier_semaphore()

    def greet_plane(i, carry):
        other = (z * NX + x + i) % (NZ * NX)
        pl.semaphore_signal(
            barrier, inc=1, device_id=dev(other % NX, y, other // NX, core), device_id_type=MESH
        )
        return carry

    def greet_line(i, carry):
        pl.semaphore_signal(
            barrier, inc=1, device_id=dev(x, (y + i) % NY, z, core), device_id_type=MESH
        )
        return carry

    lax.fori_loop(1, NZ * NX, greet_plane, 0)
    lax.fori_loop(1, NY, greet_line, 0)
    pl.semaphore_signal(barrier, inc=1, device_id=sibling, device_id_type=MESH)
    pl.semaphore_wait(barrier, NZ * NX - 1 + NY - 1 + 1)

    def band(ref, index):
        return ref.at[pl.ds(pl.multiple_of(index * BAND, BAND), BAND), :]

    def piece(zz, xh, kk, q):
        return (((zz + 2 * NZ) % NZ) * 2 + xh) * 4 + kk * 2 + q

    def held(p):
        return band(full, p)

    def arrived(p):
        copy(held(p), held(p), sib_send.at[p], full_recv.at[p], sibling).wait_recv()

    def share(p):
        copy(held(p), held(p), sib_send.at[p], full_recv.at[p], sibling).start()

    def ahead(t, p, src):
        return copy(src, held(p), z_send.at[0, t], full_recv.at[p], dev(x, y, (z + 1) % NZ, core))

    def behind(t, p, src):
        return copy(src, held(p), z_send.at[1, t], full_recv.at[p], dev(x, y, (z + NZ - 1) % NZ, core))

    def over(t, p, src):
        return copy(src, held(p), cross_send.at[t], full_recv.at[p], crossing)

    def hand(t, p):
        return copy(held(p), held(p), part_send.at[t], full_recv.at[p], partner)

    is_root = (x == 0) & (y == 0) & (z == 0)

    def piv_block(kk, xx, zz):
        return piv.at[kk, xx, pl.ds(pl.multiple_of(zz * BAND, BAND), BAND), :]

    def pan_block(kk, zz):
        return cross_pan.at[kk, pl.ds(pl.multiple_of(zz * BAND, BAND), BAND), :]

    def sup_block(xx, zz):
        return sup.at[
            pl.ds(pl.multiple_of(zz * BAND, BAND), BAND),
            pl.ds(pl.multiple_of(xx * quarter, quarter), quarter),
        ]

    def pan_src(zz):
        return pan.at[0, pl.ds(pl.multiple_of(zz * BAND, BAND), BAND), pl.ds(0, pan.shape[1])]

    def root_copies(i):
        xx, zz = i % NX, i // NX
        to = dev(xx, y, zz, core)
        return (
            copy(sup_block(xx, zz), piv_block(core, xx, zz), root_send.at[i], piv_own, to),
            copy(pan_src(zz), pan_block(core, zz), rootp_send.at[i], pan_own, to),
        )

    def y_copies(i):
        to = dev(x, (y + i) % NY, z, core)
        return (
            copy(piv_block(core, x, z), piv_block(core, x, z), y_send.at[i], piv_own, to),
            copy(pan_block(core, z), pan_block(core, z), yp_send.at[i], pan_own, to),
        )

    def z_copies(i):
        to = dev(x, y, (z + i) % NZ, core)
        return (
            copy(piv_block(core, x, z), piv_block(core, x, z), pz_send.at[i], piv_z.at[z], to),
            copy(pan_block(core, z), pan_block(core, z), pzp_send.at[i], pan_z.at[z], to),
        )

    def x_copy(i):
        xx = (x + i) % NX
        return copy(piv.at[core, x], piv.at[core, x], px_send.at[i], piv_x.at[x], dev(xx, y, z, core))

    def b_copy(xx):
        return copy(piv.at[core, xx], piv.at[core, xx], pb_send.at[xx], piv_b.at[xx], sibling)

    def bp_copy():
        return copy(cross_pan.at[core], cross_pan.at[core], pbp_send, pan_b, sibling)

    def each(first, last, make, act):
        def step(i, carry):
            made = make(i)
            for one in made if isinstance(made, tuple) else (made,):
                act(one)
            return carry

        lax.fori_loop(first, last, step, 0)

    @pl.when(is_root)
    def _():
        each(1, NZ * NX, root_copies, lambda c: c.start())
        pltpu.make_async_copy(sup_block(0, 0), piv_block(core, 0, 0), piv_own).start()
        pltpu.make_async_copy(pan_src(0), pan_block(core, 0), pan_own).start()

    ahead(0, piece(z, x_hi, core, 0), band(tgt, core * 2)).start()
    behind(0, piece(z, x_hi, core, 1), band(tgt, core * 2 + 1)).start()
    over(0, piece(z, x_hi, core, x_lo), band(tgt, core * 2 + x_lo)).start()
    mine = tgt.shape[0]
    full[pl.ds(pl.multiple_of(col * mine, mine), mine), :] = tgt[...]
    side = 2 * x_lo - 1

    def come_over(t):
        return piece(z - side * t, 1 - x_hi, core, 1 - x_lo)

    def come_by(t):
        return piece(z + side * t, 1 - x_hi, core, x_lo)

    def take_over(t):
        p = come_over(t)
        arrived(p)
        hand(t, p).start()
        share(p)

    def take_by(t):
        p = come_by(t)
        arrived(p)
        share(p)

    def ring(t, carry):
        p0 = piece(z - t, x_hi, core, 0)
        p1 = piece(z + t, x_hi, core, 1)
        arrived(p0)

        @pl.when(t < NZ - 1)
        def _():
            ahead(t, p0, held(p0)).start()

        arrived(p1)

        @pl.when(t < NZ - 1)
        def _():
            behind(t, p1, held(p1)).start()

        pc = piece(z + side * t, x_hi, core, x_lo)
        over(t, pc, held(pc)).start()
        share(p0)
        share(p1)
        take_over(t - 1)

        @pl.when(t >= 2)
        def _():
            take_by(t - 2)

        return carry

    lax.fori_loop(1, 4, ring, 0)

    own_piv = copy(piv_block(core, x, z), piv_block(core, x, z), y_send.at[0], piv_own, sibling)
    own_pan = copy(pan_block(core, z), pan_block(core, z), yp_send.at[0], pan_own, sibling)

    @pl.when(y == 0)
    def _():
        own_piv.wait_recv()
        own_pan.wait_recv()
        each(1, NY, y_copies, lambda c: c.start())

    lax.fori_loop(4, 6, ring, 0)

    @pl.when(y > 0)
    def _():
        own_piv.wait_recv()
        own_pan.wait_recv()

    each(1, NZ, z_copies, lambda c: c.start())
    lax.fori_loop(6, NZ, ring, 0)
    take_over(NZ - 1)
    take_by(NZ - 2)
    take_by(NZ - 1)

    def from_z(i):
        zz = (z + i) % NZ
        return (
            copy(piv_block(core, x, zz), piv_block(core, x, zz), pz_send.at[i], piv_z.at[zz], sibling),
            copy(pan_block(core, zz), pan_block(core, zz), pzp_send.at[i], pan_z.at[zz], sibling),
        )

    each(1, NZ, from_z, lambda c: c.wait_recv())
    each(1, NX, x_copy, lambda c: c.start())
    b_copy(x).start()
    bp_copy().start()

    def sibling_target(i, carry):
        s = (col + i) % (2 * NZ)
        arrived(s * 4 + (1 - core) * 2)
        arrived(s * 4 + (1 - core) * 2 + 1)
        return carry

    lax.fori_loop(1, 2 * NZ, sibling_target, 0)

    chunk = 256
    chunks = full.shape[0] // chunk

    def rows_of(i):
        return pl.ds(pl.multiple_of(i * chunk, chunk), chunk)

    def strip(i, carry):
        kern[rows_of(i), :] = jnp.exp(scale * dot_t(full[rows_of(i), :], sup[...]))
        return carry

    lax.fori_loop(0, chunks, strip, 0)

    def from_x(i):
        xx = (x + i) % NX
        copy(piv.at[core, xx], piv.at[core, xx], px_send.at[i], piv_x.at[xx], sibling).wait_recv()
        return b_copy(xx)

    each(1, NX, from_x, lambda c: c.start())

    def from_b(xx):
        return copy(piv.at[1 - core, xx], piv.at[1 - core, xx], pb_send.at[xx], piv_b.at[xx], sibling)

    each(0, NX, from_b, lambda c: c.wait_recv())
    copy(cross_pan.at[1 - core], cross_pan.at[1 - core], pbp_send, pan_b, sibling).wait_recv()

    width = inv.shape[1]
    span = sup.shape[0]
    here = pl.ds(pl.multiple_of(col * span, span), span)

    def out_copy(c):
        return copy(
            sol.at[pl.ds(pl.multiple_of(c * mine, mine), mine), :],
            out.at[:, here], out_send.at[c], out_recv.at[col], (row, c),
        )

    def solve(i, carry):
        number = (z // 2 + 2 + i) % chunks
        these = rows_of(number)

        def pivot_kernel(kk):
            total = jnp.zeros((chunk, width), jnp.float32)
            for xx in range(NX):
                total += dot_t(full[these, xx * quarter : (xx + 1) * quarter], piv[kk, xx])
            return jnp.exp(scale * total)

        first = dot_t(pivot_kernel(0), inv[0], HIGH)
        left = pivot_kernel(1) - jnp.dot(
            first, cross_pan[1], precision=HIGH, preferred_element_type=jnp.float32
        )
        second = dot_t(left, inv[1], HIGH)
        done = (
            kern[these, :]
            - jnp.dot(first, pan[0], precision=HIGH, preferred_element_type=jnp.float32)
            - jnp.dot(second, pan[1], precision=HIGH, preferred_element_type=jnp.float32)
        )
        head = jnp.where(
            (row == 0) & (col == 0), first,
            jnp.where((row == 1) & (col == 0), second, done[:, :width]),
        )
        sol[these, :width] = head
        sol[these, width:] = done[:, width:]
        for j in range(chunk // mine):
            c = number * (chunk // mine) + j

            @pl.when(c != col)
            def _():
                out_copy(c).start()

            @pl.when(c == col)
            def _():
                pltpu.make_async_copy(
                    sol.at[pl.ds(pl.multiple_of(c * mine, mine), mine), :],
                    out.at[:, here], out_recv.at[col],
                ).start()

        return carry

    lax.fori_loop(0, chunks, solve, 0)

    def end_ring(t, carry):
        ahead(t, 0, held(0)).wait_send()
        behind(t, 0, held(0)).wait_send()
        return carry

    lax.fori_loop(0, NZ - 1, end_ring, 0)

    def end_x(t, carry):
        over(t, 0, held(0)).wait_send()
        hand(t, 0).wait_send()
        return carry

    lax.fori_loop(0, NZ, end_x, 0)

    def end_share(i, carry):
        s = (col + i) % (2 * NZ)
        for q in range(2):
            p = s * 4 + core * 2 + q
            copy(held(p), held(p), sib_send.at[p], full_recv.at[p], sibling).wait_send()
        return carry

    lax.fori_loop(1, 2 * NZ, end_share, 0)

    @pl.when(is_root)
    def _():
        each(1, NZ * NX, root_copies, lambda c: c.wait_send())

    @pl.when(y == 0)
    def _():
        each(1, NY, y_copies, lambda c: c.wait_send())

    each(1, NZ, z_copies, lambda c: c.wait_send())
    each(1, NX, x_copy, lambda c: c.wait_send())
    each(0, NX, b_copy, lambda c: c.wait_send())
    bp_copy().wait_send()

    def end_out(i, carry):
        c = (col + i) % (2 * NZ)
        out_copy(c).wait_send()
        copy(
            sol.at[pl.ds(0, mine), :],
            out.at[:, pl.ds(pl.multiple_of(c * span, span), span)],
            out_send.at[c], out_recv.at[c], (row, c),
        ).wait_recv()
        return carry

    lax.fori_loop(1, 2 * NZ, end_out, 0)
    pltpu.make_async_copy(
        sol.at[pl.ds(pl.multiple_of(col * mine, mine), mine), :], out.at[:, here], out_recv.at[col]
    ).wait()


def shards(support, targets, panels, diag_inverses):
    span, feat = support.shape
    mine = targets.shape[0]
    width = diag_inverses.shape[1]
    n_col = 2 * NZ
    scale = 0.5 / math.sqrt(feat)
    dma = pltpu.SemaphoreType.DMA

    def kernel(*refs):
        body(scale, *refs)

    return pl.pallas_call(
        kernel,
        out_shape=jax.ShapeDtypeStruct((mine, span * n_col), jnp.float32),
        in_specs=[pl.BlockSpec(memory_space=pltpu.VMEM)] * 4,
        out_specs=pl.BlockSpec(memory_space=pl.ANY),
        scratch_shapes=[
            pltpu.VMEM((mine * n_col, feat), jnp.bfloat16),
            pltpu.VMEM((2, NX, width, feat // NX), jnp.bfloat16),
            pltpu.VMEM((2, width, width), jnp.float32),
            pltpu.VMEM((mine * n_col, span), jnp.float32),
            pltpu.VMEM((mine * n_col, span), jnp.float32),
            dma((4 * n_col,)), dma((2, NZ)), dma((NZ,)), dma((NZ,)), dma((4 * n_col,)),
            dma, dma((NZ,)), dma((NX,)), dma((NX,)),
            dma((NZ * NX,)), dma((NY,)), dma((NZ,)), dma((NX,)), dma((NX,)),
            dma, dma((NZ,)), dma, dma((NZ * NX,)), dma((NY,)), dma((NZ,)), dma,
            dma((n_col,)), dma((n_col,)),
        ],
        compiler_params=pltpu.CompilerParams(
            collective_id=0, has_side_effects=True, vmem_limit_bytes=48 * 1024 * 1024
        ),
    )(support, targets, panels, diag_inverses)


def solution(mesh):
    in_specs = (P(("row", "col"), None), P("col", None), P(None, None, ("row", "col")), P())
    out_specs = P("col", "row")
    return jax.shard_map(shards, mesh=mesh, in_specs=in_specs, out_specs=out_specs, check_vma=False)
```

time: 433 us -> 123 us (0.28)
  blocking collectives: 210 us -> 0 us
  waiting for transfers between devices: 181 us -> 0 us
  Pallas kernels: 0 us -> 117 us
  matrix products: 14.1 us -> 0 us
  between operations: 13.5 us -> 0.01 us
    psum x2 -> x0, blocking collectives: 210 us -> none  [spread(): return lax.psum(jnp.where(mine, value, jnp.zeros_like(value)), axis)]
    all_gather x2 -> x0, waiting for transfers between devices: 149 us -> none  [the longest x1 149 us: shards(): lax.all_gather(targets, 'col', axis=0, tiled=True)]
    pallas_call x0 -> x1, Pallas kernels: none -> 117 us  [shards(): pl.pallas_call(kernel, out_shape=jax.ShapeDtypeStruct((mine, span * n_col...]
    all_to_all x1 -> x0, waiting for transfers between devices: 29.8 us -> none  [shards(): lax.all_to_all(strip_tile, 'col', split_axis=0, concat_axis=1, tiled=True)]
    dot_general x5 -> x0, matrix products: 14.1 us -> none  [the longest x2 6.85 us: apply_panel(): jnp.dot(solved_head, panel_cols, precision=lax.Precision.HIGHEST, preferr...]
  transfers between devices with their start and end apart: 3 -> 0, of which waited for: 2 -> 0; matrix products, arithmetic and copies ran while one was open for 2% -> 0% of each run, Pallas kernels for 0% -> 0%
where the time goes in v1:
time: 123 us
  Pallas kernels  117 us (95%)
  local copies, waits for them, and re-layouts  5.46 us (4%)
    pallas_call x1, Pallas kernels, shards(): pl.pallas_call(kernel, out_shape=jax.ShapeDtypeStruct((mine, span * n_col...  117 us
    unnamed x9, local copies, waits for them, and re-layouts  5.46 us

profile of v1, /device:TPU:1, one launch (start us, length us, event | category | flops | bytes accessed | tf_op | source)
XLA Modules:
  0.0 122.6 jit_solution(12435859994364506072)
XLA Ops:
  0.0 0.0 copy-start
  0.0 1.6 %copy-done = bf16[256,4096]{1,0:T(8,128)(2,1)S(1)} copy-done((bf16[256,4096]{1,0:T(8,128)(2,1)S(1)}, bf16[256,4096]{1,0:T(8,128)(2,1)}, u32[]{:S(2)}) %copy-start) | copy-done | bytes 2097176
  1.6 0.0 copy-start.1
  1.6 1.0 copy-done.1
  2.6 0.0 copy-start.2
  2.6 0.9 copy-done.2
  3.6 0.0 copy-start.3
  3.6 0.9 copy-done.3
  4.5 117.1 %shard_map.46 = f32[64,4096]{1,0:T(8,128)S(1)} custom-call(bf16[256,4096]{1,0:T(8,128)(2,1)S(1)} %copy-done, bf16[64,4096]{1,0:T(8,128)(2,1)S(1)} %copy-done.1, f32[2,128,256]{2,1,0:T(8,128)S(1)} %copy-done.2, f32[2,128,128]{2,1,0:T(8,128)S(1)} %copy-done.3), custom_call_target="tpu_custom_call" | custom-call | tf_op jit(solution)/shard_map/pallas_call | solution.py:400
  121.6 1.0 copy.6
Async XLA Ops:
  0.0 1.6 %copy-start = (bf16[256,4096]{1,0:T(8,128)(2,1)S(1)}, bf16[256,4096]{1,0:T(8,128)(2,1)}, u32[]{:S(2)}) copy-start(bf16[256,4096]{1,0:T(8,128)(2,1)} %refs_0_.1) | copy-start | bytes 6291460
  1.6 1.0 copy-start.1
  2.6 0.9 copy-start.2
  3.6 0.9 copy-start.3

commit v2 on v1

v2 whole, which is shorter than its diff:
```python
import functools
import math

import jax
import jax.numpy as jnp
from jax import lax
from jax.experimental import pallas as pl
from jax.experimental.pallas import tpu as pltpu
from jax.sharding import PartitionSpec as P

MESH = pl.DeviceIdType.MESH
NZ, NY, NX = 8, 8, 4
BAND = 16
STEP_ROWS = 256
BEGIN_AT, FIRST_AT, OTHER_AT, LINE_AT, LINE_STEPS = 6, 8, 9, 12, (14, 16, 100, 101)
HIGH = lax.Precision.HIGHEST


def dot_t(a, b, precision=None):
    return lax.dot_general(
        a, b, (((1,), (1,)), ((), ())), precision=precision, preferred_element_type=jnp.float32
    )


def body(
    scale, sup_hbm, tgt, pan_hbm, inv_hbm, out,
    sup, pan, inv, full, piv, cross_pan, kern, sol,
    load, full_recv, z_send, cross_send, part_send, sib_send,
    landed, stage_recv, line_send, linep_send,
    piv_own, piv_z, piv_y, piv_b, root_send, px_send, pz_send, py_send, pb_send,
    pan_own, pan_z, pan_b, rootp_send, pxp_send, pzp_send, pbp_send,
    out_recv, out_send,
):
    row = lax.axis_index("row")
    col = lax.axis_index("col")
    core = row % 2
    y = (row // 2) % NY
    x_lo = row // (2 * NY)
    z = col // 2
    x_hi = col % 2
    x = x_hi * 2 + x_lo
    part = sup.shape[1] // NY
    half = sup.shape[1] // 2
    width = inv.shape[1]

    def dev(xx, yy, zz, kk):
        return ((xx % 2) * (2 * NY) + yy * 2 + kk, zz * 2 + xx // 2)

    sibling = dev(x, y, z, 1 - core)
    crossing = dev(NX - 1 - x, y, z, core)
    partner = dev(x_hi * 2 + 1 - x_lo, y, z, core)

    def copy(src, dst, send, recv, to):
        return pltpu.make_async_remote_copy(
            src_ref=src, dst_ref=dst, send_sem=send, recv_sem=recv, device_id=to, device_id_type=MESH
        )

    mine = tgt.shape[0]
    loads = [
        pltpu.make_async_copy(sup_hbm, sup, load.at[0]),
        pltpu.make_async_copy(pan_hbm, pan, load.at[1]),
        pltpu.make_async_copy(inv_hbm, inv, load.at[2]),
        pltpu.make_async_copy(tgt, full.at[pl.ds(pl.multiple_of(col * mine, mine), mine), :], load.at[3]),
    ]
    for one in loads:
        one.start()

    def first_x(zz):
        return (zz % 2) * (zz % NX)

    is_root = (x == 0) & (y == 0) & (z == 0)
    is_first = x == first_x(z)

    barrier = pltpu.get_barrier_semaphore()

    def greet_plane(i, carry):
        other = (z * NX + x + i) % (NZ * NX)
        pl.semaphore_signal(
            barrier, inc=1, device_id=dev(other % NX, y, other // NX, core), device_id_type=MESH
        )
        return carry

    def greet_line(i, carry):
        pl.semaphore_signal(
            barrier, inc=1, device_id=dev(x, (y + i) % NY, z, core), device_id_type=MESH
        )
        return carry

    lax.fori_loop(1, NZ * NX, greet_plane, 0)
    lax.fori_loop(1, NY, greet_line, 0)
    pl.semaphore_signal(barrier, inc=1, device_id=sibling, device_id_type=MESH)

    pl.semaphore_wait(barrier, NZ * NX - 1 + NY - 1 + 1)

    def band(ref, index, c):
        return ref.at[pl.ds(pl.multiple_of(index * BAND, BAND), BAND), pl.ds(pl.multiple_of(c * half, half), half)]

    def piece(zz, xh, kk, q):
        return (((zz + 2 * NZ) % NZ) * 2 + xh) * 4 + kk * 2 + q

    def held(p, c):
        return band(full, p, c)

    def sib(p, c):
        return copy(held(p, c), held(p, c), sib_send.at[p, c], full_recv.at[p, c], sibling)

    def arrived(p, c):
        sib(p, c).wait_recv()

    def share(p, c):
        sib(p, c).start()

    def ahead(t, p, c, src):
        return copy(src, held(p, c), z_send.at[0, t, c], full_recv.at[p, c], dev(x, y, (z + 1) % NZ, core))

    def behind(t, p, c, src):
        return copy(src, held(p, c), z_send.at[1, t, c], full_recv.at[p, c], dev(x, y, (z + NZ - 1) % NZ, core))

    def over(t, p, c, src):
        return copy(src, held(p, c), cross_send.at[t, c], full_recv.at[p, c], crossing)

    def hand(t, p, c):
        return copy(held(p, c), held(p, c), part_send.at[t, c], full_recv.at[p, c], partner)

    def piv_block(kk, yy, zz):
        return piv.at[yy, pl.ds(pl.multiple_of(kk * width + zz * BAND, BAND), BAND), :]

    def pan_block(kk, zz):
        return cross_pan.at[kk, pl.ds(pl.multiple_of(zz * BAND, BAND), BAND), :]

    def sup_band(zz):
        return sup_hbm.at[pl.ds(pl.multiple_of(zz * BAND, BAND), BAND), :]

    def staged(yy):
        return landed.at[:, pl.ds(pl.multiple_of(yy * part, part), part)]

    def pan_src(zz):
        return pan_hbm.at[0, pl.ds(pl.multiple_of(zz * BAND, BAND), BAND), pl.ds(0, inv.shape[1])]

    def root_copy(zz):
        return copy(sup_band(zz), landed, root_send.at[zz], stage_recv, dev(first_x(zz), 0, zz, core))

    def rootp_copy(zz):
        return copy(pan_src(zz), pan_block(core, zz), rootp_send.at[zz], pan_own, dev(first_x(zz), 0, zz, core))

    def line_copy(i):
        return copy(staged(i), piv_block(core, i, z), line_send.at[i], piv_own, dev(x, i, z, core))

    def linep_copy(i):
        return copy(pan_block(core, z), pan_block(core, z), linep_send.at[i], pan_own, dev(x, i, z, core))

    def x_copy(i):
        to = dev((x + i) % NX, y, z, core)
        return copy(piv_block(core, y, z), piv_block(core, y, z), px_send.at[i], piv_own, to)

    def xp_copy(i):
        to = dev((x + i) % NX, y, z, core)
        return copy(pan_block(core, z), pan_block(core, z), pxp_send.at[i], pan_own, to)

    def z_copy(i):
        to = dev(x, y, (z + i) % NZ, core)
        return copy(piv_block(core, y, z), piv_block(core, y, z), pz_send.at[i], piv_z.at[z], to)

    def zp_copy(i):
        to = dev(x, y, (z + i) % NZ, core)
        return copy(pan_block(core, z), pan_block(core, z), pzp_send.at[i], pan_z.at[z], to)

    hb = width // 2

    def piv_half(kk, yy, c):
        return piv.at[yy, pl.ds(pl.multiple_of(kk * width + c * hb, hb), hb), :]

    def y_copy(way, t, c):
        yy = (y + NY - t) % NY if way == 0 else (y + t) % NY
        to = dev(x, (y + 1) % NY if way == 0 else (y + NY - 1) % NY, z, core)
        return copy(piv_half(core, yy, c), piv_half(core, yy, c), py_send.at[way, t, c], piv_y.at[yy, c], to)

    def b_copy(yy, c):
        return copy(piv_half(core, yy, c), piv_half(core, yy, c), pb_send.at[yy, c], piv_b.at[yy, c], sibling)

    def bp_copy():
        return copy(cross_pan.at[core], cross_pan.at[core], pbp_send, pan_b, sibling)

    def each(first, last, make, act):
        def step(i, carry):
            made = make(i)
            for one in made if isinstance(made, tuple) else (made,):
                act(one)
            return carry

        lax.fori_loop(first, last, step, 0)

    @pl.when(is_root)
    def _():
        each(1, NZ, root_copy, lambda c: c.start())
        pltpu.make_async_copy(sup_band(0), landed, stage_recv).start()
        each(1, NZ, rootp_copy, lambda c: c.start())
        pltpu.make_async_copy(pan_src(0), pan_block(core, 0), pan_own).start()

    for c in range(2):
        ahead(0, piece(z, x_hi, core, 0), c, band(tgt, core * 2, c)).start()
        behind(0, piece(z, x_hi, core, 1), c, band(tgt, core * 2 + 1, c)).start()
        over(0, piece(z, x_hi, core, x_lo), c, band(tgt, core * 2 + x_lo, c)).start()
    side = 2 * x_lo - 1

    def take_over(t, c):
        p = piece(z - side * t, 1 - x_hi, core, 1 - x_lo)
        arrived(p, c)
        hand(t, p, c).start()
        share(p, c)

    def take_by(t, c):
        p = piece(z + side * t, 1 - x_hi, core, x_lo)
        arrived(p, c)
        share(p, c)

    def ring(u, carry):
        t, c = u // 2, u % 2
        p0 = piece(z - t, x_hi, core, 0)
        p1 = piece(z + t, x_hi, core, 1)
        arrived(p0, c)

        @pl.when(t < NZ - 1)
        def _():
            ahead(t, p0, c, held(p0, c)).start()

        arrived(p1, c)

        @pl.when(t < NZ - 1)
        def _():
            behind(t, p1, c, held(p1, c)).start()

        pc = piece(z + side * t, x_hi, core, x_lo)
        over(t, pc, c, held(pc, c)).start()
        share(p0, c)
        share(p1, c)
        take_over(t - 1, c)

        @pl.when(t >= 2)
        def _():
            take_by(t - 2, c)

        return carry

    own_piv = copy(piv_block(core, y, z), piv_block(core, y, z), px_send.at[0], piv_own, sibling)
    own_pan = copy(pan_block(core, z), pan_block(core, z), pxp_send.at[0], pan_own, sibling)

    def stage_begin():
        @pl.when(is_first & (y == 0))
        def _():
            pltpu.make_async_copy(sup_band(0), landed, stage_recv).wait()
            each(1, NY, line_copy, lambda c: c.start())
            pltpu.make_async_copy(staged(0), piv_block(core, 0, z), piv_own).start()
            own_pan.wait_recv()
            each(1, NY, linep_copy, lambda c: c.start())

    def stage_first():
        @pl.when(is_first)
        def _():
            own_piv.wait_recv()
            each(1, NX, x_copy, lambda c: c.start())
            each(1, NZ, z_copy, lambda c: c.start())

    def stage_other():
        @pl.when(x != first_x(z))
        def _():
            own_piv.wait_recv()
            each(1, NZ, z_copy, lambda c: c.start())

    def from_z(i):
        zz = (z + i) % NZ
        return copy(piv_block(core, y, zz), piv_block(core, y, zz), pz_send.at[i], piv_z.at[zz], sibling)

    def fromp_z(i):
        zz = (z + i) % NZ
        return copy(pan_block(core, zz), pan_block(core, zz), pzp_send.at[i], pan_z.at[zz], sibling)

    def stage_line():
        each(1, NZ, from_z, lambda c: c.wait_recv())
        for c in range(2):
            y_copy(0, 0, c).start()
            y_copy(1, 0, c).start()
        for c in range(2):
            b_copy(y, c).start()

        @pl.when(is_first & (y > 0))
        def _():
            own_pan.wait_recv()

        @pl.when(is_first)
        def _():
            each(1, NX, xp_copy, lambda c: c.start())

        @pl.when(x != first_x(z))
        def _():
            own_pan.wait_recv()

        each(1, NZ, zp_copy, lambda c: c.start())

    def y_step(t):
        for c in range(2):
            for way in range(2):
                if t < NY // 2 or c == way:
                    one = y_copy(way, t, c)
                    one.wait_recv()
                    if t < NY // 2 - 1 or (t == NY // 2 - 1 and c == way):
                        one.start()
                    b_copy((y + NY - t) % NY if way == 0 else (y + t) % NY, c).start()

    def ring_end(u):
        t, c = u // 2, u % 2
        take_over(t - 1, c)
        take_by(t - 2, c)

    stages = [(BEGIN_AT, stage_begin), (FIRST_AT, stage_first), (OTHER_AT, stage_other), (LINE_AT, stage_line)]
    stages += [(at, functools.partial(y_step, 1 + n)) for n, at in enumerate(LINE_STEPS)]
    done = 2
    for at, stage in sorted(stages, key=lambda one: one[0]):
        upto = min(at, 2 * NZ)
        if upto > done:
            lax.fori_loop(done, upto, lambda u, carry: ring(u, carry), 0)
            done = upto
        while done < at:
            if done < 2 * NZ + 2:
                ring_end(done)
            done += 1
        if at < 100:
            stage()
    for u in range(done, 2 * NZ + 2):
        ring_end(u)
    for c in range(2):
        take_by(NZ - 1, c)

    def sibling_target(i, carry):
        s = (col + i) % (2 * NZ)
        for q in range(2):
            for c in range(2):
                arrived(s * 4 + (1 - core) * 2 + q, c)
        return carry

    lax.fori_loop(1, 2 * NZ, sibling_target, 0)
    for one in loads:
        one.wait()

    chunk = 256
    chunks = full.shape[0] // chunk

    def rows_of(i):
        return pl.ds(pl.multiple_of(i * chunk, chunk), chunk)

    def strip(i, carry):
        kern[rows_of(i), :] = jnp.exp(scale * dot_t(full[rows_of(i), :], sup[...]))
        return carry

    def from_b(yy, c):
        return copy(piv_half(1 - core, yy, c), piv_half(1 - core, yy, c), pb_send.at[yy, c], piv_b.at[yy, c], sibling)

    for i in range(chunks):
        for n, at in enumerate(LINE_STEPS):
            if at == 100 + i:
                y_step(1 + n)
        strip(i, 0)
    each(1, NZ, fromp_z, lambda c: c.wait_recv())
    bp_copy().start()
    each(0, 2 * NY, lambda i: from_b(i // 2, i % 2), lambda c: c.wait_recv())
    copy(cross_pan.at[1 - core], cross_pan.at[1 - core], pbp_send, pan_b, sibling).wait_recv()

    span = sup.shape[0]
    here = pl.ds(pl.multiple_of(col * span, span), span)

    def out_copy(c):
        return copy(
            sol.at[pl.ds(pl.multiple_of(c * mine, mine), mine), :],
            out.at[:, here], out_send.at[c], out_recv.at[col], (row, c),
        )

    step_rows = STEP_ROWS
    steps = full.shape[0] // step_rows

    def solve(i, carry):
        number = (z * 2 * mine // step_rows + steps // 2 + i) % steps
        these = pl.ds(pl.multiple_of(number * step_rows, step_rows), step_rows)

        total = jnp.zeros((step_rows, 2 * width), jnp.float32)
        for yy in range(NY):
            total += dot_t(full[these, yy * part : (yy + 1) * part], piv[yy])
        pivots = jnp.exp(scale * total)
        first = dot_t(pivots[:, :width], inv[0], HIGH)
        left = pivots[:, width:] - jnp.dot(
            first, cross_pan[1], precision=HIGH, preferred_element_type=jnp.float32
        )
        second = dot_t(left, inv[1], HIGH)
        done = (
            kern[these, :]
            - jnp.dot(
                jnp.concatenate([first, second], axis=1), pan[...].reshape(2 * width, span),
                precision=HIGH, preferred_element_type=jnp.float32,
            )
        )
        head = jnp.where(
            (row == 0) & (col == 0), first,
            jnp.where((row == 1) & (col == 0), second, done[:, :width]),
        )
        sol[these, :width] = head
        sol[these, width:] = done[:, width:]
        for j in range(step_rows // mine):
            c = number * (step_rows // mine) + j

            @pl.when(c != col)
            def _():
                out_copy(c).start()

            @pl.when(c == col)
            def _():
                pltpu.make_async_copy(
                    sol.at[pl.ds(pl.multiple_of(c * mine, mine), mine), :],
                    out.at[:, here], out_recv.at[col],
                ).start()

        return carry

    lax.fori_loop(0, steps, solve, 0)

    def end_ring(u, carry):
        t, c = u // 2, u % 2
        ahead(t, 0, c, held(0, c)).wait_send()
        behind(t, 0, c, held(0, c)).wait_send()
        return carry

    lax.fori_loop(0, 2 * NZ - 2, end_ring, 0)

    def end_x(u, carry):
        t, c = u // 2, u % 2
        over(t, 0, c, held(0, c)).wait_send()
        hand(t, 0, c).wait_send()
        return carry

    lax.fori_loop(0, 2 * NZ, end_x, 0)

    def end_share(i, carry):
        s = (col + i) % (2 * NZ)
        for q in range(2):
            for c in range(2):
                sib(s * 4 + core * 2 + q, c).wait_send()
        return carry

    lax.fori_loop(1, 2 * NZ, end_share, 0)

    @pl.when(is_root)
    def _():
        each(1, NZ, root_copy, lambda c: c.wait_send())
        each(1, NZ, rootp_copy, lambda c: c.wait_send())

    @pl.when(is_first & (y == 0))
    def _():
        each(1, NY, line_copy, lambda c: c.wait_send())
        each(1, NY, linep_copy, lambda c: c.wait_send())

    @pl.when(is_first)
    def _():
        each(1, NX, x_copy, lambda c: c.wait_send())
        each(1, NX, xp_copy, lambda c: c.wait_send())

    each(1, NZ, z_copy, lambda c: c.wait_send())
    each(1, NZ, zp_copy, lambda c: c.wait_send())
    for t in range(NY // 2):
        for c in range(2):
            for way in range(2):
                if t < NY // 2 - 1 or c == way:
                    y_copy(way, t, c).wait_send()
    each(0, 2 * NY, lambda i: b_copy(i // 2, i % 2), lambda c: c.wait_send())
    bp_copy().wait_send()

    def end_out(i, carry):
        c = (col + i) % (2 * NZ)
        out_copy(c).wait_send()
        copy(
            sol.at[pl.ds(0, mine), :],
            out.at[:, pl.ds(pl.multiple_of(c * span, span), span)],
            out_send.at[c], out_recv.at[c], (row, c),
        ).wait_recv()
        return carry

    lax.fori_loop(1, 2 * NZ, end_out, 0)
    pltpu.make_async_copy(
        sol.at[pl.ds(pl.multiple_of(col * mine, mine), mine), :], out.at[:, here], out_recv.at[col]
    ).wait()


def shards(support, targets, panels, diag_inverses):
    span, feat = support.shape
    mine = targets.shape[0]
    width = diag_inverses.shape[1]
    n_col = 2 * NZ
    scale = 0.5 / math.sqrt(feat)
    dma = pltpu.SemaphoreType.DMA

    def kernel(*refs):
        body(scale, *refs)

    return pl.pallas_call(
        kernel,
        out_shape=jax.ShapeDtypeStruct((mine, span * n_col), jnp.float32),
        in_specs=[pl.BlockSpec(memory_space=pltpu.HBM)] * 4,
        out_specs=pl.BlockSpec(memory_space=pltpu.HBM),
        scratch_shapes=[
            pltpu.VMEM(support.shape, support.dtype),
            pltpu.VMEM(panels.shape, panels.dtype),
            pltpu.VMEM(diag_inverses.shape, diag_inverses.dtype),
            pltpu.VMEM((mine * n_col, feat), jnp.bfloat16),
            pltpu.VMEM((NY, 2 * width, feat // NY), jnp.bfloat16),
            pltpu.VMEM((2, width, width), jnp.float32),
            pltpu.VMEM((mine * n_col, span), jnp.float32),
            pltpu.VMEM((mine * n_col, span), jnp.float32),
            dma((4,)), dma((4 * n_col, 2)), dma((2, NZ, 2)), dma((NZ, 2)), dma((NZ, 2)), dma((4 * n_col, 2)),
            pltpu.VMEM((BAND, feat), jnp.bfloat16), dma, dma((NY,)), dma((NY,)),
            dma, dma((NZ,)), dma((NY, 2)), dma((NY, 2)),
            dma((NZ,)), dma((NX,)), dma((NZ,)), dma((2, NY, 2)), dma((NY, 2)),
            dma, dma((NZ,)), dma, dma((NZ,)), dma((NX,)), dma((NZ,)), dma,
            dma((n_col,)), dma((n_col,)),
        ],
        compiler_params=pltpu.CompilerParams(
            collective_id=0, has_side_effects=True, vmem_limit_bytes=67_000_000
        ),
    )(support, targets, panels, diag_inverses)


def solution(mesh):
    in_specs = (P(("row", "col"), None), P("col", None), P(None, None, ("row", "col")), P())
    out_specs = P("col", "row")
    return jax.shard_map(shards, mesh=mesh, in_specs=in_specs, out_specs=out_specs, check_vma=False)
```

time: 123 us -> 104 us (0.85); the launches traced: 123 us -> 102 us
  Pallas kernels: 117 us -> 99.9 us
  local copies, waits for them, and re-layouts: 5.46 us -> 2.27 us
    pallas_call x1, Pallas kernels: 117 us -> 99.9 us  [shards(): pl.pallas_call(kernel, out_shape=jax.ShapeDtypeStruct((mine, span * n_col...]
    unnamed x9 -> x1, local copies, waits for them, and re-layouts: 5.46 us -> 2.27 us
where the time goes in v2:
time: 104 us; the launch traced here: 102 us
  Pallas kernels  99.9 us (96%)
  local copies, waits for them, and re-layouts  2.27 us (2%)
    pallas_call x1, Pallas kernels, shards(): pl.pallas_call(kernel, out_shape=jax.ShapeDtypeStruct((mine, span * n_col...  99.9 us
    unnamed x1, local copies, waits for them, and re-layouts  2.27 us

profile of v2, /device:TPU:1, one launch (start us, length us, event | category | flops | bytes accessed | tf_op | source)
XLA Modules:
  0.0 102.1 jit_solution(8087571286601635256)
XLA Ops:
  0.0 99.9 %shard_map.46 = f32[64,4096]{1,0:T(8,128)} custom-call(bf16[256,4096]{1,0:T(8,128)(2,1)} %refs_0_.1, bf16[64,4096]{1,0:T(8,128)(2,1)} %refs_1_.1, f32[2,128,256]{2,1,0:T(8,128)} %refs_2_.1, f32[2,128,128]{2,1,0:T(8,128)} %refs_3_.1), custom_call_target="tpu_custom_call" | custom-call | tf_op jit(solution)/shard_map/pallas_call | solution.py:501
  99.9 2.3 %copy.6 = f32[64,4096]{1,0:T(8,128)} copy(f32[64,4096]{1,0:T(8,128)} %shard_map.46) | data formatting | bytes 2097152

commit v3 on v2

--- a/solution.py
+++ b/solution.py
@@ -360,8 +360,9 @@
             if at == 100 + i:
                 y_step(1 + n)
         strip(i, 0)
-    each(1, NZ, fromp_z, lambda c: c.wait_recv())
-    bp_copy().start()
+        if i == 1:
+            each(1, NZ, fromp_z, lambda c: c.wait_recv())
+            bp_copy().start()
     each(0, 2 * NY, lambda i: from_b(i // 2, i % 2), lambda c: c.wait_recv())
     copy(cross_pan.at[1 - core], cross_pan.at[1 - core], pbp_send, pan_b, sibling).wait_recv()
 

time: 104 us -> 103 us (level)
  no operation moved by 1% of the time
where the time goes in v3:
time: 103 us; the launch traced here: 102 us
  Pallas kernels  99.4 us (97%)
  local copies, waits for them, and re-layouts  2.27 us (2%)
    pallas_call x1, Pallas kernels, shards(): pl.pallas_call(kernel, out_shape=jax.ShapeDtypeStruct((mine, span * n_col...  99.4 us
    unnamed x1, local copies, waits for them, and re-layouts  2.27 us

profile of v3, /device:TPU:1, one launch (start us, length us, event | category | flops | bytes accessed | tf_op | source)
XLA Modules:
  0.0 101.7 jit_solution(12965796182049852021)
XLA Ops:
  0.0 99.4 %shard_map.46 = f32[64,4096]{1,0:T(8,128)} custom-call(bf16[256,4096]{1,0:T(8,128)(2,1)} %refs_0_.1, bf16[64,4096]{1,0:T(8,128)(2,1)} %refs_1_.1, f32[2,128,256]{2,1,0:T(8,128)} %refs_2_.1, f32[2,128,128]{2,1,0:T(8,128)} %refs_3_.1), custom_call_target="tpu_custom_call" | custom-call | tf_op jit(solution)/shard_map/pallas_call | solution.py:502
  99.4 2.3 %copy.6 = f32[64,4096]{1,0:T(8,128)} copy(f32[64,4096]{1,0:T(8,128)} %shard_map.46) | data formatting | bytes 2097152
